TPU v7x, 256 devices: a whole 4x4x8 slice. The times are simulated.
256 devices in a mesh: fsdp: 16 (over y, x), ctx: 16 (over z, core).
Axes of the slice: x: 4, y: 4, z: 8, core: 2. Of those that a mesh axis runs over, the one named last changes fastest.
Arguments:
- queries: bfloat16 [32768, 2048], P(('fsdp', 'ctx')), may hold values from -80 to 80
- keys: bfloat16 [32768, 2048], P(('fsdp', 'ctx')), may hold values from -4 to 4
- values: bfloat16 [32768, 2048], P(('fsdp', 'ctx')), may hold values from -6 to 6
- out_weight: bfloat16 [2048, 4096], P('fsdp'), may hold values from -0.125 to 0.125
- sessions: int32 [16, 2048], P('fsdp'), may hold values from 0 to 2, never falling along the last dimension, each value on 1 to 1536 neighbouring positions
Outputs:
- output: bfloat16 [32768, 4096], P(('fsdp', 'ctx'))
Inputs may be any that keep to these rules, and one draw needn't show every extreme that they name: Along each slab the session number never falls; each of the 3 sessions holds 1 to 1536 tokens and one holds exactly 1536.
All inputs are finite; a program needn't handle non-finite values.
Results may differ from a plain program's by a relative error of at most 0.007.
Values may be sent and summed in bfloat16 or wider, within the bound.
No kernel may reach another device: no remote copies, remote signals or barrier semaphores. Data moves between devices by JAX's collectives and lax.ppermute only.
A program may use at most 128 MiB of HBM per device.

v0:
```python
import math
import jax
import jax.numpy as jnp
from jax import lax
from jax.sharding import PartitionSpec as P

HDIM = 128


def per_device(queries, keys, values, out_weight, sessions):
    tokens_here = queries.shape[0]
    width = queries.shape[1]
    heads_here = width // HDIM
    scale = 1.0 / math.sqrt(HDIM)
    slab_ids = sessions[0]
    first_token = lax.axis_index("ctx") * tokens_here
    my_positions = first_token + jnp.arange(tokens_here, dtype=jnp.int32)
    my_ids = lax.dynamic_slice_in_dim(slab_ids, first_token, tokens_here)
    query_heads = jnp.transpose(queries.reshape(tokens_here, heads_here, HDIM), (1, 0, 2))
    start_state = (
        jnp.full((heads_here, tokens_here), -1e30, jnp.float32),
        jnp.zeros((heads_here, tokens_here), jnp.float32),
        jnp.zeros((heads_here, tokens_here, HDIM), jnp.float32),
    )
    key_piece = lax.all_gather(keys, "ctx", axis=0, tiled=True)
    value_piece = lax.all_gather(values, "ctx", axis=0, tiled=True)
    count = key_piece.shape[0]
    key_positions = jnp.arange(count, dtype=jnp.int32)
    allowed = (my_ids[:, None] == slab_ids[None, :]) & (
        key_positions[None, :] <= my_positions[:, None]
    )

    def update(current):
        key_heads = jnp.transpose(key_piece.reshape(count, heads_here, HDIM), (1, 0, 2))
        value_heads = jnp.transpose(value_piece.reshape(count, heads_here, HDIM), (1, 0, 2))

        def one_head(operands):
            query_head, key_head, value_head, row_max, row_total, accum = operands
            scores = jnp.dot(query_head, key_head.T, preferred_element_type=jnp.float32) * scale
            scores = jnp.where(allowed, scores, jnp.float32(-1e30))
            new_max = jnp.maximum(row_max, jnp.max(scores, axis=1))
            weights = jnp.where(allowed, jnp.exp(scores - new_max[:, None]), jnp.float32(0.0))
            factor = jnp.exp(row_max - new_max)
            new_total = row_total * factor + jnp.sum(weights, axis=1)
            added = jnp.dot(
                weights.astype(jnp.bfloat16), value_head, preferred_element_type=jnp.float32
            )
            return (new_max, new_total, accum * factor[:, None] + added)

        return lax.map(one_head, (query_heads, key_heads, value_heads) + tuple(current))

    row_max, row_total, accum = lax.cond(
        jnp.any(allowed), update, lambda current: current, start_state
    )
    finished = accum / row_total[:, :, None]
    attended = jnp.transpose(finished, (1, 0, 2)).reshape(tokens_here, width).astype(jnp.bfloat16)
    piece = lax.all_gather(out_weight, "fsdp", axis=0, tiled=True)
    projected = jnp.dot(attended, piece, preferred_element_type=jnp.float32)
    return projected.astype(jnp.bfloat16)


def solution(mesh):
    return jax.shard_map(
        per_device,
        mesh=mesh,
        in_specs=(
            P(("fsdp", "ctx"), None),
            P(("fsdp", "ctx"), None),
            P(("fsdp", "ctx"), None),
            P("fsdp", None),
            P("fsdp", None),
        ),
        out_specs=P(("fsdp", "ctx"), None),
        check_vma=False,
    )
```

profile of v0, /device:TPU:1, one launch (start us, length us, event | category | flops | bytes accessed | tf_op | source)
XLA Modules:
  0.0 274.5 jit_solution(3808026801106439446)
XLA Ops:
  6.5 2.0 copy.8
  8.7 2.0 copy.9
  12.1 1.7 fusion.16
  15.7 63.8 %all-gather.4.cloned.1.call-done = bf16[2048,2048]{0,1:T(8,128)(2,1)} async-done(((bf16[128,2048]{0,1:T(8,128)(2,1)}), bf16[2048,2048]{0,1:T(8,128)(2,1)}) %all-gather.4.cloned.1.call-update) | async-done | bytes 8388624 | tf_op jit(solution)/shard_map/all_gather | solution.py:25
  79.5 64.4 %all-gather.6.cloned.1.call-done = bf16[2048,2048]{0,1:T(8,128)(2,1)} async-done(((bf16[128,2048]{0,1:T(8,128)(2,1)}), bf16[2048,2048]{0,1:T(8,128)(2,1)}) %all-gather.6.cloned.1.call-update) | async-done | bytes 8388624 | tf_op jit(solution)/shard_map/all_gather | solution.py:26
  143.9 86.1 %conditional.1 = (f32[16,128]{1,0:T(8,128)}, f32[16,128,128]{1,2,0:T(8,128)}) conditional(s32[]{:T(128)} %convert_element_type.18, () %tuple.17, (bf16[2048,2048]{0,1:T(8,128)(2,1)}, bf16[2048,2048]{0,1:T(8,128)(2,1)}, bf16[16,128,128]{1,2,0:T(8,128)(2,1)S(1)}, pred[128,2048]{1,0:T(32,128)(4,1)S(1)}) %tuple.49), branch_computations={%region_1.0_spmd, %region_2.7_spmd} | conditional | flops 136593792 | bytes 5349073 | solution.py:52
  143.9 86.1 %while.11 = (s32[]{:T(128)}, f32[16,128]{1,0:T(8,128)}, f32[16,128,128]{1,2,0:T(8,128)}, bf16[16,128,128]{1,2,0:T(8,128)(2,1)S(1)}, bf16[16,2048,128]{1,2,0:T(8,...) while((s32[]{:T(128)}, f32[16,128]{1,0:T(8,128)}, ...), condition=%wide.region_6.6_spmd, body=%wide.region_3.5_spmd.sunk | while | flops 136593792 | bytes 5348977 | solution.py:50
  143.9 1.5 fusion.28
  149.3 1.5 fusion.28
  154.7 1.5 fusion.28
  160.1 1.5 fusion.28
  165.5 1.5 fusion.28
  170.9 1.5 fusion.28
  176.2 1.5 fusion.28
  181.6 1.5 fusion.28
  192.4 1.5 fusion.28
  197.7 1.5 fusion.28
  203.1 1.5 fusion.28
  208.5 1.5 fusion.28
  213.9 1.5 fusion.28
  219.3 1.5 fusion.28
  224.7 1.5 fusion.28
  231.4 27.4 %all-gather.8.cloned.1.call-done = bf16[2048,4096]{1,0:T(8,128)(2,1)} async-done(((bf16[128,4096]{1,0:T(8,128)(2,1)}), bf16[2048,4096]{1,0:T(8,128)(2,1)}) %all-gather.8.cloned.1.call-update) | async-done | bytes 16777232 | tf_op jit(solution)/shard_map/all_gather | solution.py:57
  258.8 9.1 %convolution_convert_fusion = bf16[128,4096]{1,0:T(8,128)(2,1)} fusion(bf16[128,2048]{0,1:T(8,128)(2,1)S(1)} %bitcast.45, bf16[2048,4096]{1,0:T(8,128)(2,1)} %all-gather.8.cloned.1.call-done), kind=kOutput, calls=%fused_computation.22 | convolution fusion | flops 2148007936 | bytes 18350080 | tf_op jit(solution)/shard_map/dot_general | solution.py:58
  (125 shorter events, 67.7 us)
Async XLA Ops:
  6.5 73.0 %all-gather.4.cloned.1.call-start = ((), (), s32[]{:S(2)}) async-start(), calls=%async_computation | async-start | bytes 8912896 | tf_op jit(solution)/shard_map/all_gather | solution.py:25
  8.6 135.3 %all-gather.6.cloned.1.call-start = ((), (), s32[]{:S(2)}) async-start(), calls=%async_computation.1 | async-start | bytes 8912896 | tf_op jit(solution)/shard_map/all_gather | solution.py:26
  10.7 248.1 %all-gather.8.cloned.1.call-start = ((), (), s32[]{:S(2)}) async-start(), calls=%async_computation.2 | async-start | bytes 17825792 | tf_op jit(solution)/shard_map/all_gather | solution.py:57
Sparse Core Ops, SparseCore 0:
  9.1 70.3 all-gather.3
  81.2 62.6 all-gather.5
  146.4 112.4 all-gather.7
where the time goes:
time: 277 us; the launch traced here: 274 us
  waiting for transfers between devices  156 us (56%)
  matrix products  56 us (20%)
  local copies, waits for them, and re-layouts  38.5 us (14%)
  between operations  13.7 us (5%)
  other arithmetic  9.54 us (3%)
    all_gather x1, waiting for transfers between devices, per_device(): value_piece = lax.all_gather(values, 'ctx', axis=0, tiled=True)  64.4 us
    all_gather x1, waiting for transfers between devices, per_device(): key_piece = lax.all_gather(keys, 'ctx', axis=0, tiled=True)  63.8 us
    dynamic_update_slice x48, local copies, waits for them, and re-layouts, update(): lax.map(one_head, (query_heads, key_heads, value_heads) + tuple(current))  32.4 us
    all_gather x1, waiting for transfers between devices, per_device(): piece = lax.all_gather(out_weight, 'fsdp', axis=0, tiled=True)  27.4 us
    dot_general x16, matrix products, one_head(): jnp.dot(query_head, key_head.T, preferred_element_type=jnp.float32) * scale  23.7 us
    dot_general x16, matrix products, one_head(): jnp.dot(weights.astype(jnp.bfloat16), value_head, preferred_element_type=...  23.2 us
    dot_general x1, matrix products, per_device(): projected = jnp.dot(attended, piece, preferred_element_type=jnp.float32)  9.1 us
    reduce_sum x16, other arithmetic, one_head(): new_total = row_total * factor + jnp.sum(weights, axis=1)  6.21 us
  transfers between devices with their start and end apart: 3, of which 3 were waited for; matrix products, arithmetic and copies ran while one was open for 34% of the time, Pallas kernels for 0%

commit v1 on v0

--- a/solution.py
+++ b/solution.py
@@ -54,7 +54,9 @@
     )
     finished = accum / row_total[:, :, None]
     attended = jnp.transpose(finished, (1, 0, 2)).reshape(tokens_here, width).astype(jnp.bfloat16)
-    piece = lax.all_gather(out_weight, "fsdp", axis=0, tiled=True)
+    piece = jnp.concatenate(
+        lax.all_to_all(jnp.stack([out_weight] * lax.axis_size("fsdp")), "fsdp", 0, 0), axis=0
+    )
     projected = jnp.dot(attended, piece, preferred_element_type=jnp.float32)
     return projected.astype(jnp.bfloat16)
 

time: 277 us -> 293 us (1.058)
  matrix products: 56 us -> 66.3 us
  starting transfers between devices: 0.09 us -> 7.81 us
  local copies, waits for them, and re-layouts: 38.5 us -> 31.5 us
  waiting for transfers between devices: 156 us -> 163 us
    all_to_all x0 -> x1, waiting for transfers between devices: none -> 47.5 us  [per_device(): lax.all_to_all(jnp.stack([out_weight] * lax.axis_size('fsdp')), 'fsdp', 0...]
    all_gather x1 -> x0, waiting for transfers between devices: 27.4 us -> none  [per_device(): piece = lax.all_gather(out_weight, 'fsdp', axis=0, tiled=True)]
    all_gather x1, waiting for transfers between devices: 63.8 us -> 51.1 us  [per_device(): key_piece = lax.all_gather(keys, 'ctx', axis=0, tiled=True)]
    dynamic_update_slice x48 -> x16, local copies, waits for them, and re-layouts: 32.4 us -> 20.3 us  [update(): lax.map(one_head, (query_heads, key_heads, value_heads) + tuple(current))]
    dot_general x16, matrix products: 23.2 us -> 33.3 us  [one_head(): jnp.dot(weights.astype(jnp.bfloat16), value_head, preferred_element_type=...]
    all_to_all x0 -> x1, starting transfers between devices: none -> 7.77 us  [per_device(): lax.all_to_all(jnp.stack([out_weight] * lax.axis_size('fsdp')), 'fsdp', 0...]
    another operation x0 -> x1, local copies, waits for them, and re-layouts: none -> 6.81 us  [per_device(): jnp.stack([out_weight] * lax.axis_size('fsdp'))]
  transfers between devices with their start and end apart: 3 -> 3, of which waited for: 3 -> 3; matrix products, arithmetic and copies ran while one was open for 34% -> 32% of each run, Pallas kernels for 0% -> 0%
where the time goes in v1:
time: 293 us; the launch traced here: 290 us
  waiting for transfers between devices  163 us (56%)
  matrix products  66.3 us (23%)
  local copies, waits for them, and re-layouts  31.5 us (11%)
  between operations  14.1 us (5%)
  starting transfers between devices  7.81 us (3%)
  other arithmetic  7.57 us (3%)
    all_gather x1, waiting for transfers between devices, per_device(): value_piece = lax.all_gather(values, 'ctx', axis=0, tiled=True)  64.3 us
    all_gather x1, waiting for transfers between devices, per_device(): key_piece = lax.all_gather(keys, 'ctx', axis=0, tiled=True)  51.1 us
    all_to_all x1, waiting for transfers between devices, per_device(): lax.all_to_all(jnp.stack([out_weight] * lax.axis_size('fsdp')), 'fsdp', 0...  47.5 us
    dot_general x16, matrix products, one_head(): jnp.dot(weights.astype(jnp.bfloat16), value_head, preferred_element_type=...  33.3 us
    dot_general x16, matrix products, one_head(): jnp.dot(query_head, key_head.T, preferred_element_type=jnp.float32) * scale  23.6 us
    dynamic_update_slice x16, local copies, waits for them, and re-layouts, update(): lax.map(one_head, (query_heads, key_heads, value_heads) + tuple(current))  20.3 us
    dot_general x1, matrix products, per_device(): projected = jnp.dot(attended, piece, preferred_element_type=jnp.float32)  9.49 us
    all_to_all x1, starting transfers between devices, per_device(): lax.all_to_all(jnp.stack([out_weight] * lax.axis_size('fsdp')), 'fsdp', 0...  7.77 us
  transfers between devices with their start and end apart: 3, of which 3 were waited for; matrix products, arithmetic and copies ran while one was open for 32% of the time, Pallas kernels for 0%

profile of v1, /device:TPU:1, one launch (start us, length us, event | category | flops | bytes accessed | tf_op | source)
XLA Modules:
  0.0 290.5 jit_solution(2970328275958009456)
XLA Ops:
  10.7 6.8 %stack.2 = bf16[16,128,4096]{2,1,0:T(8,128)(2,1)} broadcast(bf16[128,4096]{1,0:T(8,128)(2,1)} %param.12), dimensions={1,2} | broadcast | bytes 17825792 | tf_op jit(solution)/shard_map/stack | solution.py:58
  17.5 7.8 %all-to-all-start = ((bf16[16,128,4096]{2,1,0:T(8,128)(2,1)}), bf16[16,128,4096]{2,1,0:T(8,128)(2,1)}, u32[]{:S(2)}, u32[]{:S(2)}) async-start(bf16[16,128,4096]{2,1,0:T(8,128)(2,1)} %stack.2), calls=%async_computation | async-start | bytes 33554432 | tf_op jit(solution)/shard_map/all_to_all | solution.py:58
  27.4 51.1 %all-gather.3.cloned.1.call-done = bf16[2048,2048]{0,1:T(8,128)(2,1)} async-done(((bf16[128,2048]{0,1:T(8,128)(2,1)}), bf16[2048,2048]{0,1:T(8,128)(2,1)}) %all-gather.3.cloned.1.call-update) | async-done | bytes 8388624 | tf_op jit(solution)/shard_map/all_gather | solution.py:25
  78.5 64.3 %all-gather.5.cloned.1.call-done = bf16[2048,2048]{0,1:T(8,128)(2,1)} async-done(((bf16[128,2048]{0,1:T(8,128)(2,1)}), bf16[2048,2048]{0,1:T(8,128)(2,1)}) %all-gather.5.cloned.1.call-update) | async-done | bytes 8388624 | tf_op jit(solution)/shard_map/all_gather | solution.py:26
  142.8 83.8 %conditional.1 = (f32[16,128]{1,0:T(8,128)}, f32[16,128,128]{2,1,0:T(8,128)}) conditional(s32[]{:T(128)} %convert_element_type.16, () %tuple.17, (bf16[2048,2048]{0,1:T(8,128)(2,1)}, bf16[2048,2048]{0,1:T(8,128)(2,1)}, bf16[16,128,128]{1,2,0:T(8,128)(2,1)S(1)}, pred[128,2048]{1,0:T(32,128)(4,1)S(1)}) %tuple.45), branch_computations={%region_1.0_spmd, %region_2.7_spmd} | conditional | flops 136593792 | bytes 5087945 | solution.py:52
  142.8 83.8 %while.11 = (s32[]{:T(128)}, f32[16,128]{1,0:T(8,128)}, f32[16,128,128]{2,1,0:T(8,128)}, bf16[16,128,128]{1,2,0:T(8,128)(2,1)S(1)}, bf16[16,2048,128]{1,2,0:T(8,...) while((s32[]{:T(128)}, f32[16,128]{1,0:T(8,128)}, ...), condition=%wide.region_6.6_spmd, body=%wide.region_3.5_spmd.sunk | while | flops 136593792 | bytes 5087849 | solution.py:50
  144.7 2.1 fusion.32
  149.9 2.1 fusion.32
  155.2 2.1 fusion.32
  160.4 2.1 fusion.32
  165.6 2.1 fusion.32
  170.9 2.1 fusion.32
  176.1 2.1 fusion.32
  181.3 2.1 fusion.32
  186.5 2.1 fusion.32
  191.8 2.1 fusion.32
  197.0 2.1 fusion.32
  202.3 2.1 fusion.32
  207.5 2.1 fusion.32
  212.7 2.1 fusion.32
  218.0 2.1 fusion.32
  223.2 2.1 fusion.32
  226.6 47.5 %all-to-all-done = bf16[16,128,4096]{2,1,0:T(8,128)(2,1)} async-done(((bf16[16,128,4096]{2,1,0:T(8,128)(2,1)}), bf16[16,128,4096]{2,1,0:T(8,128)(2,1)}, u32[]{:S(2)}, u32[]{:S(2)}) %all-to-all-start) | async-done | bytes 16777248 | tf_op jit(solution)/shard_map/all_to_all | solution.py:58
  274.2 9.5 %fusion.17 = bf16[128,4096]{1,0:T(8,128)(2,1)} fusion(bf16[16,128,4096]{2,1,0:T(8,128)(2,1)} %all-to-all-done, f32[16,128,128]{2,1,0:T(8,128)} %get-tuple-element.57, f32[16,128]{1,0:T(8,128)} %get-tuple-element.58), kind=kOutput, calls=%fused_computation.23 | convolution fusion | flops 2148532224 | bytes 18882560 | tf_op jit(solution)/shard_map/dot_general | solution.py:60
  (96 shorter events, 55.9 us)
Async XLA Ops:
  6.5 72.0 %all-gather.3.cloned.1.call-start = ((), (), s32[]{:S(2)}) async-start(), calls=%async_computation.1 | async-start | bytes 8912896 | tf_op jit(solution)/shard_map/all_gather | solution.py:25
  8.6 134.2 %all-gather.5.cloned.1.call-start = ((), (), s32[]{:S(2)}) async-start(), calls=%async_computation.2 | async-start | bytes 8912896 | tf_op jit(solution)/shard_map/all_gather | solution.py:26
  17.5 7.8 %copy-start.1 = (s32[1,2048]{1,0:T(1,128)S(1)}, s32[1,2048]{1,0:T(1,128)}, u32[]{:S(2)}) copy-start(s32[1,2048]{1,0:T(1,128)} %param.13) | copy-start | bytes 24580
  17.5 9.6 %copy-start = (bf16[128,2048]{1,0:T(8,128)(2,1)S(1)}, bf16[128,2048]{1,0:T(8,128)(2,1)}, u32[]{:S(2)}) copy-start(bf16[128,2048]{1,0:T(8,128)(2,1)} %param.9) | copy-start | bytes 1572868
  17.5 256.6 %all-to-all-start = ((bf16[16,128,4096]{2,1,0:T(8,128)(2,1)}), bf16[16,128,4096]{2,1,0:T(8,128)(2,1)}, u32[]{:S(2)}, u32[]{:S(2)}) async-start(bf16[16,128,4096]{2,1,0:T(8,128)(2,1)} %stack.2), calls=%async_computation | async-start | bytes 33554432 | tf_op jit(solution)/shard_map/all_to_all | solution.py:58
Sparse Core Ops, SparseCore 0:
  9.1 69.3 all-gather.2
  80.3 62.5 all-gather.4
